TPU v7x, 32 devices: a whole 2x2x4 slice. The times are simulated.
32 devices in a mesh: img: 2 (over core), band: 4 (over z), pw: 4 (over y, x).
Axes of the slice: x: 2, y: 2, z: 4, core: 2. Of those that a mesh axis runs over, the one named last changes fastest.
Arguments:
- coefficients: bfloat16 [2, 1024, 32, 2048], P('img', None, ('band', 'pw')), may hold values from -6 to 6
- rotation: bfloat16 [2, 1024, 256], P('img'), may hold values from -0.1875 to 0.1875
- positions: int32 [2, 3, 256], P('img'), may hold values from 0 to 63, as said below
- start_pos: int32 [3, 256], replicated, may hold values from 0 to 63, as said below
- end_pos: int32 [3, 256], replicated, may hold values from 0 to 63, as said below
- species: int32 [256], replicated, may hold values from 0 to 3
- depth: float32 [4], replicated, may hold values from 0.5 to 3
Outputs:
- correction: bfloat16 [2, 256, 32, 2048], P('img', None, ('band', 'pw'))
- ritz_values: float32 [2, 256], P('img')
- band_force: float32 [2, 3, 256], P('img')
- along_force: float32 [2], P('img')
Inputs may be any that keep to these rules, and one draw needn't show every extreme that they name: `positions`: grid index of each atom's centre along each dimension. `start_pos`: grid index of each atom's centre along each dimension. `end_pos`: grid index of each atom's centre along each dimension.
All inputs are finite; a program needn't handle non-finite values.
Results may differ from a plain program's by a relative error of at most 0.012.
The roundings to bfloat16 on the way count: a program that leaves them out, or rounds other values in their place, can miss the bound.
Values may be sent and summed in bfloat16 or wider, within the bound.
A program may use at most 128 MiB of HBM per device.

v0:
```python
import math
import jax
import jax.numpy as jnp
from jax import lax
from jax.sharding import PartitionSpec as P

G = 64
W = 32
BANDS = 1024
BLOCK = 256
SPECIES = 4
kinetic_scale = 0.01
sigma_cells = 3.0
spring_constant = 2.0
epsilon = 1e-06
highest = lax.Precision.HIGHEST


def passed_along(block, axis, distance):
    devices = range(lax.axis_size(axis))
    route = [(i - distance, i) for i in devices if i - distance in devices]
    return lax.ppermute(block, axis, route)


def phases(box_order, box_size, grid_size):
    wavenum = box_order - box_size // 2
    grid_cells = jnp.arange(grid_size, dtype=jnp.int32)
    turn_count = jnp.mod(wavenum[:, None] * grid_cells[None, :], grid_size)
    return turn_count.astype(jnp.float32) * (2.0 * math.pi / grid_size)


def forward_table(box_order, box_size, grid_size):
    angle_tab = phases(box_order, box_size, grid_size)
    cosine = jnp.cos(angle_tab) / math.sqrt(box_size)
    sine_part = jnp.sin(angle_tab) / math.sqrt(box_size)
    dft_table = jnp.stack(
        [jnp.stack([cosine, sine_part], 1), jnp.stack([-sine_part, cosine], 1)], 0
    )
    return dft_table.astype(jnp.bfloat16)


def inverse_table(box_order, box_size, grid_size):
    angle_tab = phases(box_order, box_size, grid_size).T
    factor = math.sqrt(box_size) / grid_size
    cosine = jnp.cos(angle_tab) * factor
    sine_part = jnp.sin(angle_tab) * factor
    dft_table = jnp.stack(
        [jnp.stack([cosine, -sine_part], 1), jnp.stack([sine_part, cosine], 1)], 0
    )
    return dft_table.astype(jnp.bfloat16)


def section_zy(coeff_block, table_z, table_y):
    leading = coeff_block.shape[0]
    planes = coeff_block.shape[1]
    split_up = coeff_block.reshape(leading, planes, W, 2, W)
    along_z = jnp.einsum(
        "blyck,ckdn->blydn", split_up, table_z, preferred_element_type=jnp.float32
    ).astype(jnp.bfloat16)
    along_y = jnp.einsum(
        "blycz,cydm->blmdz", along_z, table_y, preferred_element_type=jnp.float32
    ).astype(jnp.bfloat16)
    return along_y.reshape(leading, planes, G * 2 * G)


def section_x(arrived, table_x):
    leading = arrived.shape[0]
    y_rows = arrived.shape[2] // (2 * G)
    split_up = arrived.reshape(leading, W, y_rows, 2, G)
    return jnp.einsum("bxycz,cxdn->bnydz", split_up, table_x, preferred_element_type=jnp.float32)


def section_x_inverse(weighted, table_x):
    leading = weighted.shape[0]
    y_rows = weighted.shape[2]
    along_x = jnp.einsum(
        "bnydz,dncx->bxycz", weighted, table_x, preferred_element_type=jnp.float32
    ).astype(jnp.bfloat16)
    return along_x.reshape(leading, W, y_rows * 2 * G)


def section_zy_inverse(returned, table_y, table_z):
    leading = returned.shape[0]
    planes = returned.shape[1]
    split_up = returned.reshape(leading, planes, G, 2, G)
    along_y = jnp.einsum(
        "blmdz,dmcy->blycz", split_up, table_y, preferred_element_type=jnp.float32
    ).astype(jnp.bfloat16)
    along_z = jnp.einsum("blydn,dnck->blyck", along_y, table_z, preferred_element_type=jnp.float32)
    return along_z.reshape(leading, planes, W * 2 * W)


def wrap_offset(values):
    return jnp.mod(values + G // 2, G) - G // 2


def gaussians(coords, grid_cells):
    offset = wrap_offset(grid_cells[None, :] - coords[:, None]).astype(jnp.float32)
    return (jnp.exp(-offset * offset / (2.0 * sigma_cells * sigma_cells)), offset)


def atom_tables(own_pos, y_cells):
    grid_cells = jnp.arange(G, dtype=jnp.int32)
    gauss_x, offset_x = gaussians(own_pos[0], grid_cells)
    gauss_y, offset_y = gaussians(own_pos[1], y_cells)
    gauss_z, offset_z = gaussians(own_pos[2], grid_cells)
    return (gauss_x, offset_x, gauss_y, offset_y, gauss_z, offset_z)


def local_potential(tables, strength):
    gauss_x, offset_x, gauss_y, offset_y, gauss_z, offset_z = tables
    atom_count = gauss_x.shape[0]
    joined = (gauss_y[:, :, None] * gauss_z[:, None, :]).reshape(atom_count, -1)
    potential = jnp.dot((strength[:, None] * gauss_x).T, joined, precision=highest)
    return (potential, joined)


def atom_forces(density, tables, joined, strength):
    gauss_x, offset_x, gauss_y, offset_y, gauss_z, offset_z = tables
    atom_count = gauss_x.shape[0]
    with_y = ((gauss_y * offset_y)[:, :, None] * gauss_z[:, None, :]).reshape(atom_count, -1)
    with_z = (gauss_y[:, :, None] * (gauss_z * offset_z)[:, None, :]).reshape(atom_count, -1)
    stacked = jnp.concatenate([joined, with_y, with_z], 0)
    moments = jnp.dot(density, stacked.T, precision=highest)
    prefactor = -strength / (sigma_cells * sigma_cells)
    force_x = prefactor * jnp.sum(gauss_x * offset_x * moments[:, :atom_count].T, 1)
    force_y = prefactor * jnp.sum(gauss_x * moments[:, atom_count : 2 * atom_count].T, 1)
    force_z = prefactor * jnp.sum(gauss_x * moments[:, 2 * atom_count :].T, 1)
    return jnp.stack([force_x, force_y, force_z], 0)


def space_work(in_space, own_pos, strength, y_rows):
    y_cells = jnp.arange(y_rows, dtype=jnp.int32)
    tables = atom_tables(own_pos, y_cells)
    potential, joined = local_potential(tables, strength)
    grid_potential = potential.reshape(G, y_rows, G)
    density = jnp.sum(in_space * in_space, axis=(0, 3)).reshape(G, y_rows * G) / BLOCK
    force_part = atom_forces(density, tables, joined, strength)
    weighted = (in_space * grid_potential[:, :, None, :]).astype(jnp.bfloat16)
    return (weighted, force_part)


def kinetic_table(x_cells):
    entries = jnp.arange(W * 2 * W, dtype=jnp.int32)
    wave_y = entries // (2 * W) - W // 2
    wave_z = jnp.mod(entries, W) - W // 2
    wave_x = x_cells - W // 2
    squared = wave_x[:, None] * wave_x[:, None] + (wave_y * wave_y + wave_z * wave_z)[None, :]
    return kinetic_scale * 0.5 * squared.astype(jnp.float32)


def rotate_quarter(values):
    leading = values.shape[0]
    middle = values.shape[1]
    split_up = values.reshape(leading, middle, W, 2, W)
    turned = jnp.stack([-split_up[:, :, :, 1, :], split_up[:, :, :, 0, :]], 3)
    return turned.reshape(values.shape)


def chain_forces(force, own_pos, before, after):
    ahead_step = wrap_offset(after - own_pos).astype(jnp.float32)
    behind = wrap_offset(own_pos - before).astype(jnp.float32)
    tangent_raw = ahead_step + behind
    entries = 3 * own_pos.shape[1]
    tangent = (
        tangent_raw * lax.rsqrt(jnp.mean(tangent_raw * tangent_raw) + epsilon) / math.sqrt(entries)
    )
    length_ahead = jnp.sqrt(entries * (jnp.mean(ahead_step * ahead_step) + epsilon))
    length_behind = jnp.sqrt(entries * (jnp.mean(behind * behind) + epsilon))
    along_path = jnp.sum(force * tangent)
    band_push = (
        force - along_path * tangent + spring_constant * (length_ahead - length_behind) * tangent
    )
    return (band_push, along_path)


def body(coefficients, rotation, positions, start_pos, end_pos, species, depth):
    coeff_all = coefficients[0]
    planes = coeff_all.shape[1]
    flat_all = coeff_all.reshape(BANDS, -1)
    orbitals = jnp.einsum("ib,ik->bk", rotation[0], flat_all, preferred_element_type=jnp.float32)
    orbitals = orbitals.astype(jnp.bfloat16).reshape(BLOCK, planes, W * 2 * W)
    kind_ids = jnp.arange(SPECIES, dtype=jnp.int32)
    strength = jnp.sum(jnp.where(species[:, None] == kind_ids[None, :], depth[None, :], 0.0), 1)
    own_pos = positions[0]
    natural = jnp.arange(W, dtype=jnp.int32)
    table_f = forward_table(natural, W, G)
    table_i = inverse_table(natural, W, G)
    whole_vectors = lax.all_to_all(
        orbitals, ("band", "pw"), split_axis=0, concat_axis=1, tiled=True
    )
    spread = section_zy(whole_vectors, table_f, table_f)
    weighted, force_part = space_work(section_x(spread, table_f), own_pos, strength, G)
    partial_apply = section_zy_inverse(section_x_inverse(weighted, table_i), table_i, table_i)
    applied = lax.all_to_all(partial_apply, ("band", "pw"), split_axis=1, concat_axis=0, tiled=True)
    x_cells = lax.axis_index(("band", "pw")) * planes + jnp.arange(planes, dtype=jnp.int32)
    kinetic = kinetic_table(x_cells)
    orbitals_wide = orbitals.astype(jnp.float32)
    hamiltonian = kinetic[None] * orbitals_wide + applied
    numerator = jnp.sum(orbitals_wide * hamiltonian, axis=(1, 2))
    denominator = jnp.sum(orbitals_wide * orbitals_wide, axis=(1, 2))
    numerator, denominator, atom_force = lax.psum(
        (numerator, denominator, force_part), ("band", "pw")
    )
    npw_total = W * W * W
    ritz_values = numerator / npw_total / (denominator / npw_total + epsilon)
    residual = hamiltonian - ritz_values[:, None, None] * orbitals_wide
    search = (residual / (1.0 + kinetic)[None]).astype(jnp.bfloat16)
    search_pair = jnp.concatenate(
        [search.reshape(BLOCK, -1), (-rotate_quarter(search)).reshape(BLOCK, -1)], 0
    )
    intersections = (
        jnp.einsum("ik,jk->ij", flat_all, search_pair, preferred_element_type=jnp.float32)
        / npw_total
    )
    intersections = lax.psum(intersections, ("band", "pw")).astype(jnp.bfloat16)
    projected = jnp.einsum("ij,ik->jk", intersections, flat_all, preferred_element_type=jnp.float32)
    projection = projected[:BLOCK].reshape(BLOCK, planes, -1) + rotate_quarter(
        projected[BLOCK:].reshape(BLOCK, planes, -1)
    )
    correction = (search.astype(jnp.float32) - projection).astype(jnp.bfloat16)
    image_idx = lax.axis_index("img")
    before = passed_along(own_pos, "img", 1)
    after = passed_along(own_pos, "img", -1)
    before = jnp.where(image_idx == 0, start_pos, before)
    after = jnp.where(image_idx == lax.axis_size("img") - 1, end_pos, after)
    band_push, along_path = chain_forces(atom_force, own_pos, before, after)
    return (correction[None], ritz_values[None], band_push[None], along_path[None])


def solution(mesh):
    in_specs = (
        P("img", None, ("band", "pw"), None),
        P("img", None, None),
        P("img", None, None),
        P(),
        P(),
        P(),
        P(),
    )
    out_specs = (
        P("img", None, ("band", "pw"), None),
        P("img", None),
        P("img", None, None),
        P("img"),
    )
    return jax.shard_map(body, mesh=mesh, in_specs=in_specs, out_specs=out_specs, check_vma=False)
```

profile of v0, /device:TPU:0, one launch (start us, length us, event | category | flops | bytes accessed | tf_op | source)
XLA Modules:
  0.0 592.1 jit_solution(8768601264481166253)
XLA Ops:
  0.6 12.1 %copy.141 = bf16[128,8,2,2048]{3,1,2,0:T(8,128)(2,1)} copy(bf16[128,8,2,2048]{3,2,1,0:T(2,128)(2,1)} %bitcast.208) | data formatting | bytes 16777216
  12.7 5.8 convolution_convert_fusion
  21.3 8.6 %all-to-all-start = ((bf16[256,2,2048]{2,1,0:T(2,128)(2,1)}), bf16[256,2,2048]{2,1,0:T(2,128)(2,1)}, u32[]{:S(2)}, u32[]{:S(2)}) async-start(bf16[256,2,2048]{2,1,0:T(2,128)(2,1)} %reshape.676), calls=%async_computation | async-start | bytes 4194304 | tf_op jit(solution)/shard_map/all_to_all | solution.py:189
  30.5 7.5 %fusion.29 = f32[64,64,64]{2,0,1:T(8,128)} fusion(f32[256,64]{0,1:T(8,128)S(1)} %get-tuple-element.67, f32[256,64]{0,1:T(8,128)S(1)} %get-tuple-element.74, s32[256]{0:T(256)S(1)} %bitcast.217, f32[256]{0:T(256)S(1)} %select_reduce_fusion), kind=kOutput, calls=%fused_computation.35 | convolution fusion | flops 806666240 | bytes 1181696 | tf_op jit(solution)/shard_map/dot_general | solution.py:114
  37.9 35.0 %all-to-all-done = bf16[256,2,2048]{2,1,0:T(2,128)(2,1)} async-done(((bf16[256,2,2048]{2,1,0:T(2,128)(2,1)}), bf16[256,2,2048]{2,1,0:T(2,128)(2,1)}, u32[]{:S(2)}, u32[]{:S(2)}) %all-to-all-start) | async-done | bytes 2097184 | tf_op jit(solution)/shard_map/all_to_all | solution.py:189
  76.9 17.9 %reshape.677 = bf16[16,32,32,2,32]{4,3,2,0,1:T(2,128)(2,1)} reshape(bf16[16,16,2,2048]{3,0,2,1:T(8,128)(2,1)} %copy.102) | data formatting | bytes 4194304 | tf_op jit(solution)/shard_map/reshape | solution.py:56
  94.8 12.6 %fusion.20 = bf16[16,32,64,2,64]{4,2,1,0,3:T(8,128)(2,1)} fusion(bf16[16,32,32,2,32,1]{4,3,2,0,1,5:T(2,128)(2,1)} %bitcast.203, bf16[1,32,2,64]{3,1,0,2:T(8,128)(2,1)S(1)} %get-tuple-element.57, bf16[1,32,2,64]{3,1,0,2:T(8,128)(2,1)S(1)} %get-tuple-element.56), kind=kOutput, calls=%fused_computation.24 | convolution fusion | flops 811663360 | bytes 10502144 | tf_op jit(solution)/shard_map/blycz,cydm->blmdz/dot_general | solution.py:60
  107.4 28.7 %fusion.1 = (f32[64,64,64]{2,0,1:T(8,128)}, bf16[16,64,64,2,64]{4,1,2,0,3:T(8,128)(2,1)}) fusion(f32[64,64,64]{2,0,1:T(8,128)} %fusion.29, bf16[16,32,64,2,64]{4,2,1,0,3:T(8,128)(2,1)} %fusion.20, bf16[1,32,2,64]{3,1,0,2:T(8,128)(2,1)S(1)} %get-tuple-element.57, bf16[1,32,2,64]{3,1,0,2:T(8,128)(2,1)S(1)} %get-tuple-element.56), kind=kOutput, calls=%fused_computation.3 | convolution fusion | flops 1107066880 | bytes 27279360 | tf_op jit(solution)/shard_map/bxycz,cxdn->bnydz/dot_general | solution.py:70
  136.1 18.9 %fusion.6 = bf16[16,32,64,2,64,1]{4,1,2,0,3,5:T(8,128)(2,1)} fusion(bf16[16,64,64,2,64]{4,1,2,0,3:T(8,128)(2,1)} %get-tuple-element.40, bf16[1,64,2,32]{1,3,0,2:T(8,128)(2,1)S(1)} %get-tuple-element.55, bf16[1,64,2,32]{1,3,0,2:T(8,128)(2,1)S(1)} %get-tuple-element.54), kind=kOutput, calls=%fused_computation.10 | convolution fusion | flops 1077968896 | bytes 25182208 | tf_op jit(solution)/shard_map/bnydz,dncx->bxycz/dot_general | solution.py:76
  155.0 19.3 %convolution_bitcast_fusion = f32[16,32,32,2,32]{4,2,3,1,0:T(8,128)} fusion(bf16[16,32,64,2,64,1]{4,1,2,0,3,5:T(8,128)(2,1)} %fusion.6, bf16[1,64,2,32]{1,3,0,2:T(8,128)(2,1)S(1)} %get-tuple-element.55, bf16[1,64,2,32]{1,3,0,2:T(8,128)(2,1)S(1)} %get-tuple-element.54), kind=kOutput, calls=%fused_computation.25 | convolution fusion | flops 807469056 | bytes 12599296 | tf_op jit(solution)/shard_map/blydn,dnck->blyck/dot_general | solution.py:89
  174.3 28.6 %copy.138 = f32[16,32,32,2,32]{4,3,2,0,1:T(2,128)} copy(f32[16,32,32,2,32]{4,2,3,1,0:T(8,128)} %convolution_bitcast_fusion) | data formatting | bytes 8388608 | tf_op jit(solution)/shard_map/reshape | solution.py:90
  202.9 21.7 %reshape.699 = f32[16,32,2048]{2,0,1:T(8,128)} reshape(f32[16,32,32,2,32]{4,3,2,0,1:T(2,128)} %copy.138) | data formatting | bytes 8388608 | tf_op jit(solution)/shard_map/reshape | solution.py:90
  224.6 10.1 %all-to-all-start.1 = ((f32[16,32,2048]{2,0,1:T(8,128)}), f32[16,32,2048]{2,0,1:T(8,128)}, u32[]{:S(2)}, u32[]{:S(2)}) async-start(f32[16,32,2048]{2,0,1:T(8,128)} %reshape.699), calls=%async_computation.1 | async-start | bytes 8388608 | tf_op jit(solution)/shard_map/all_to_all | solution.py:195
  239.4 5.0 broadcast_multiply_fusion.2
  247.5 5.1 reshape.682
  263.4 12.6 %fusion.14 = f32[64,768]{1,0:T(8,128)S(1)} fusion(f32[64,4096]{1,0:T(8,128)} %div.129, f32[256,4096]{0,1:T(8,128)} %bitcast.212, f32[256,4096]{0,1:T(8,128)} %bitcast.213, f32[256,4096]{0,1:T(8,128)} %bitcast.211), kind=kOutput, calls=%fused_computation.18 | convolution fusion | flops 2422210560 | bytes 13828096 | tf_op jit(solution)/shard_map/dot_general | solution.py:124
  276.2 36.9 %all-to-all-done.1 = f32[16,32,2048]{2,0,1:T(8,128)} async-done(((f32[16,32,2048]{2,0,1:T(8,128)}), f32[16,32,2048]{2,0,1:T(8,128)}, u32[]{:S(2)}, u32[]{:S(2)}) %all-to-all-start.1) | async-done | bytes 4194336 | tf_op jit(solution)/shard_map/all_to_all | solution.py:195
  313.0 5.5 copy.110
  318.5 4.7 copy.109
  323.2 5.9 %copy.143 = f32[32,8,2,2048]{3,1,2,0:T(8,128)} copy(f32[32,8,2,2048]{3,2,1,0:T(2,128)S(1)} %bitcast.206) | data formatting | bytes 8388608
  329.1 18.0 %all_to_all.36 = f32[256,2,32,2,32]{4,3,2,0,1:T(2,128)} reshape(f32[16,16,2,2048]{3,1,0,2:T(8,128)} %copy.109) | data formatting | bytes 8388608 | tf_op jit(solution)/shard_map/all_to_all | solution.py:195
  347.1 20.8 %copy.114 = f32[256,2,32,2,32]{0,4,3,2,1:T(8,128)} copy(f32[256,2,32,2,32]{4,3,2,0,1:T(2,128)} %all_to_all.36) | data formatting | bytes 8388608 | tf_op jit(solution)/shard_map/all_to_all | solution.py:195
  371.1 54.3 %all-reduce.1 = (f32[256]{0:T(256)S(1)}, f32[256]{0:T(256)S(1)}) all-reduce(f32[256]{0:T(256)S(1)} %get-tuple-element.25, f32[256]{0:T(256)S(1)} %get-tuple-element.24), channel_id=1, replica_groups=mesh['img'=2,'band'=4,'pw'=4] {'band','pw'}, use_global_device_ids=true, to_apply=%region_4.5 | all-reduce | flops 512 | bytes 4096 | tf_op jit(solution)/shard_map/psum | solution.py:202
  425.5 4.6 fusion.41
  435.7 8.2 %multiply_bitcast_fusion = f32[1024,512]{0,1:T(8,128)S(1)} fusion(bf16[1024,4096]{1,0:T(8,128)(2,1)} %bitcast.199, bf16[256,4096]{1,0:T(8,128)(2,1)} %copy.115, bf16[256,4096]{1,0:T(8,128)(2,1)} %fusion.41), kind=kOutput, calls=%fused_computation.59 | convolution fusion | flops 4303880192 | bytes 14680064 | tf_op jit(solution)/shard_map/ik,jk->ij/dot_general | solution.py:213
  444.0 97.9 %all-reduce.3 = (bf16[1024,512]{0,1:T(8,128)(2,1)}, f32[3,256]{1,0:T(4,128)S(1)}) all-reduce(f32[1024,512]{0,1:T(8,128)S(1)} %multiply_bitcast_fusion, f32[3,256]{1,0:T(4,128)S(1)} %pad_maximum_fusion.9), channel_id=1, replica_groups=mesh['img'=2,'band'=4,'pw'=4] {'band','pw'}, use_global_device_ids=true, to_apply=%region_5.6 | all-reduce | flops 525056 | bytes 3151872 | tf_op jit(solution)/shard_map/psum | solution.py:216
  543.7 7.2 %fusion.152 = f32[512,4096]{1,0:T(8,128)S(1)} fusion(bf16[1024,512]{0,1:T(8,128)(2,1)} %get-tuple-element.29, bf16[1024,4096]{1,0:T(8,128)(2,1)} %bitcast.200), kind=kOutput, calls=%fused_computation.217 | convolution fusion | flops 4294967296 | bytes 17825792 | tf_op jit(solution)/shard_map/ij,ik->jk/dot_general | solution.py:217
  550.9 3.8 fusion.146
  554.6 5.6 copy.116
  565.5 5.4 copy.118
  570.9 6.6 %reshape.680 = f32[1,256,2,2048]{3,2,1,0:T(2,128)} reshape(f32[256,4096]{1,0:T(8,128)} %get-tuple-element.41) | data formatting | bytes 8388608 | tf_op jit(solution)/shard_map/reshape | solution.py:218
  577.4 10.7 %fusion.35 = bf16[1,256,2,2048]{3,1,2,0:T(8,128)(2,1)S(1)} fusion(f32[1,256,2,2048]{3,1,2,0:T(8,128)} %copy.118, f32[1,256,2,2048]{3,2,1,0:T(2,128)} %reshape.680, f32[16,16,2,2048]{3,1,0,2:T(8,128)} %copy.109, f32[1,256,2,2048]{3,2,1,0:T(2,128)} %reshape.682, f32[2,2048]{1,0:T(2,128)S(1)} %get-tuple-element.53, f32[256]{0:T(256)S(1)} %add_divide_fusion, ...), kind=kLoop, calls=%fused_computation.43 | loop fusion | flops 10485760 | bytes 18908160 | tf_op jit(solution)/shard_map/convert_element_type | solution.py:221
  (66 shorter events, 42.6 us)
Async XLA Ops:
  0.6 12.1 %copy-start = (bf16[1,1024,256]{2,1,0:T(8,128)(2,1)S(1)}, bf16[1,1024,256]{2,1,0:T(8,128)(2,1)}, u32[]{:S(2)}) copy-start(bf16[1,1024,256]{2,1,0:T(8,128)(2,1)} %param.8) | copy-start | bytes 1572868
  18.5 11.8 %copy-start.8 = (s32[256]{0:T(256)S(1)}, s32[256]{0:T(256)}, u32[]{:S(2)}) copy-start(s32[256]{0:T(256)} %param.12) | copy-start | bytes 3076
  18.5 11.8 %copy-start.9 = (f32[4]{0:T(128)S(1)}, f32[4]{0:T(128)}, u32[]{:S(2)}) copy-start(f32[4]{0:T(128)} %param.13) | copy-start | bytes 52
  18.5 11.9 %copy-start.4 = (s32[1,3,256]{2,0,1:T(1,128)S(1)}, s32[1,3,256]{2,0,1:T(1,128)}, u32[]{:S(2)}) copy-start(s32[1,3,256]{2,0,1:T(1,128)} %param.9) | copy-start | bytes 9220
  21.3 51.6 %all-to-all-start = ((bf16[256,2,2048]{2,1,0:T(2,128)(2,1)}), bf16[256,2,2048]{2,1,0:T(2,128)(2,1)}, u32[]{:S(2)}, u32[]{:S(2)}) async-start(bf16[256,2,2048]{2,1,0:T(2,128)(2,1)} %reshape.676), calls=%async_computation | async-start | bytes 4194304 | tf_op jit(solution)/shard_map/all_to_all | solution.py:189
  224.6 88.5 %all-to-all-start.1 = ((f32[16,32,2048]{2,0,1:T(8,128)}), f32[16,32,2048]{2,0,1:T(8,128)}, u32[]{:S(2)}, u32[]{:S(2)}) async-start(f32[16,32,2048]{2,0,1:T(8,128)} %reshape.699), calls=%async_computation.1 | async-start | bytes 8388608 | tf_op jit(solution)/shard_map/all_to_all | solution.py:195
  234.7 18.0 %collective-permute-start = (s32[3,256]{1,0:T(4,128)S(1)}, s32[3,256]{1,0:T(4,128)S(1)}, u32[]{:S(2)}, u32[]{:S(2)}) collective-permute-start(s32[3,256]{1,0:T(4,128)S(1)} %bitcast.224), channel_id=1, source_target_pairs={{16,0},{17,1},{18,2},{19,3},{20,4},{21,5},{22,6},{23,7},{24,8},{25... | collective-permute-start | bytes 9224 | tf_op jit(solution)/shard_map/ppermute | solution.py:22
  236.0 16.7 %collective-permute-start.1 = (s32[3,256]{1,0:T(4,128)S(1)}, s32[3,256]{1,0:T(4,128)S(1)}, u32[]{:S(2)}, u32[]{:S(2)}) collective-permute-start(s32[3,256]{1,0:T(4,128)S(1)} %bitcast.225), channel_id=1, source_target_pairs={{0,16},{1,17},{2,18},{3,19},{4,20},{5,21},{6,22},{7,23},{8,24},{9,... | collective-permute-start | bytes 9224 | tf_op jit(solution)/shard_map/ppermute | solution.py:22
  247.5 5.2 copy-start.6
  247.5 5.2 copy-start.7
  425.5 151.9 %copy-start.5 = (f32[256]{0:T(256)}, f32[256]{0:T(256)S(1)}, u32[]{:S(2)}) copy-start(f32[256]{0:T(256)S(1)} %add_divide_fusion) | copy-start | bytes 3076
  425.5 4.7 copy-start.2
  425.5 5.5 copy-start.3
  577.4 14.2 %copy-start.1 = (bf16[1,1024,256]{2,1,0:T(8,128)(2,1)S(1)}, bf16[1,1024,256]{2,1,0:T(8,128)(2,1)}, u32[]{:S(2)}) copy-start(bf16[1,1024,256]{2,1,0:T(8,128)(2,1)} %param.8) | copy-start | bytes 1572868
where the time goes:
time: 600 us; the launch traced here: 592 us
  local copies, waits for them, and re-layouts  185 us (31%)
  blocking collectives  152 us (25%)
  matrix products  121 us (20%)
  waiting for transfers between devices  71.8 us (12%)
  other arithmetic  35.2 us (6%)
  starting transfers between devices  23 us (4%)
    psum x1, blocking collectives, body(): intersections = lax.psum(intersections, ('band', 'pw')).astype(jnp.bfloat16)  97.9 us
    psum x1, blocking collectives, body(): lax.psum((numerator, denominator, force_part), ('band', 'pw'))  54.3 us
    reshape x2, local copies, waits for them, and re-layouts, section_zy_inverse(): return along_z.reshape(leading, planes, W * 2 * W)  50.3 us
    all_to_all x4, local copies, waits for them, and re-layouts, body(): lax.all_to_all(partial_apply, ('band', 'pw'), split_axis=1, concat_axis=0...  48.9 us
    all_to_all x1, waiting for transfers between devices, body(): lax.all_to_all(partial_apply, ('band', 'pw'), split_axis=1, concat_axis=0...  36.9 us
    all_to_all x1, waiting for transfers between devices, body(): lax.all_to_all(orbitals, ('band', 'pw'), split_axis=0, concat_axis=1, til...  35 us
    dot_general x1, matrix products, section_x(): jnp.einsum('bxycz,cxdn->bnydz', split_up, table_x, preferred_element_type...  28.7 us
    unnamed x26, local copies, waits for them, and re-layouts  22.4 us
  transfers between devices with their start and end apart: 4, of which 2 were waited for; matrix products, arithmetic and copies ran while one was open for 7% of the time, Pallas kernels for 0%

commit v1 on v0

--- a/solution.py
+++ b/solution.py
@@ -200,7 +200,7 @@
     numerator = jnp.sum(orbitals_wide * hamiltonian, axis=(1, 2))
     denominator = jnp.sum(orbitals_wide * orbitals_wide, axis=(1, 2))
     numerator, denominator, atom_force = lax.psum(
-        (numerator, denominator, force_part), ("band", "pw")
+        lax.psum((numerator, denominator, force_part), "pw"), "band"
     )
     npw_total = W * W * W
     ritz_values = numerator / npw_total / (denominator / npw_total + epsilon)

time: 600 us -> 577 us (0.962)
  blocking collectives: 152 us -> 132 us
    psum x1 -> x2, blocking collectives: 54.3 us -> 34.6 us  [the longest x1 19.3 us: body(): lax.psum(lax.psum((numerator, denominator, force_part), 'pw'), 'band')]
    unnamed x26 -> x28, local copies, waits for them, and re-layouts: 22.4 us -> 22.4 us
  transfers between devices with their start and end apart: 4 -> 4, of which waited for: 2 -> 2; matrix products, arithmetic and copies ran while one was open for 7% -> 8% of each run, Pallas kernels for 0% -> 0%
where the time goes in v1:
time: 577 us; the launch traced here: 570 us
  local copies, waits for them, and re-layouts  185 us (32%)
  blocking collectives  132 us (23%)
  matrix products  121 us (21%)
  waiting for transfers between devices  71.8 us (12%)
  other arithmetic  33.1 us (6%)
  starting transfers between devices  23 us (4%)
    psum x1, blocking collectives, body(): intersections = lax.psum(intersections, ('band', 'pw')).astype(jnp.bfloat16)  97.3 us
    reshape x2, local copies, waits for them, and re-layouts, section_zy_inverse(): return along_z.reshape(leading, planes, W * 2 * W)  50.3 us
    all_to_all x4, local copies, waits for them, and re-layouts, body(): lax.all_to_all(partial_apply, ('band', 'pw'), split_axis=1, concat_axis=0...  48.9 us
    all_to_all x1, waiting for transfers between devices, body(): lax.all_to_all(partial_apply, ('band', 'pw'), split_axis=1, concat_axis=0...  36.9 us
    all_to_all x1, waiting for transfers between devices, body(): lax.all_to_all(orbitals, ('band', 'pw'), split_axis=0, concat_axis=1, til...  35 us
    dot_general x1, matrix products, section_x(): jnp.einsum('bxycz,cxdn->bnydz', split_up, table_x, preferred_element_type...  28.7 us
    unnamed x28, local copies, waits for them, and re-layouts  22.4 us
    psum x1, blocking collectives, body(): lax.psum(lax.psum((numerator, denominator, force_part), 'pw'), 'band')  19.3 us
  transfers between devices with their start and end apart: 4, of which 2 were waited for; matrix products, arithmetic and copies ran while one was open for 8% of the time, Pallas kernels for 0%

profile of v1, /device:TPU:0, one launch (start us, length us, event | category | flops | bytes accessed | tf_op | source)
XLA Modules:
  0.0 569.7 jit_solution(11406081001757413797)
XLA Ops:
  0.6 12.1 %copy.141 = bf16[128,8,2,2048]{3,1,2,0:T(8,128)(2,1)} copy(bf16[128,8,2,2048]{3,2,1,0:T(2,128)(2,1)} %bitcast.208) | data formatting | bytes 16777216
  12.7 5.8 %convolution_convert_fusion = bf16[256,4096]{1,0:T(8,128)(2,1)S(1)} fusion(bf16[1024,4096]{1,0:T(8,128)(2,1)} %bitcast.198, bf16[1,1024,256]{2,1,0:T(8,128)(2,1)S(1)} %copy-done), kind=kOutput, calls=%fused_computation.29 | convolution fusion | flops 2148532224 | bytes 11010048 | tf_op jit(solution)/shard_map/ib,ik->bk/dot_general | solution.py:181
  21.3 8.6 %all-to-all-start = ((bf16[256,2,2048]{2,1,0:T(2,128)(2,1)}), bf16[256,2,2048]{2,1,0:T(2,128)(2,1)}, u32[]{:S(2)}, u32[]{:S(2)}) async-start(bf16[256,2,2048]{2,1,0:T(2,128)(2,1)} %reshape.676), calls=%async_computation | async-start | bytes 4194304 | tf_op jit(solution)/shard_map/all_to_all | solution.py:189
  30.5 7.5 %fusion.29 = f32[64,64,64]{2,0,1:T(8,128)} fusion(f32[256,64]{0,1:T(8,128)S(1)} %get-tuple-element.69, f32[256,64]{0,1:T(8,128)S(1)} %get-tuple-element.76, s32[256]{0:T(256)S(1)} %bitcast.217, f32[256]{0:T(256)S(1)} %select_reduce_fusion), kind=kOutput, calls=%fused_computation.35 | convolution fusion | flops 806666240 | bytes 1181696 | tf_op jit(solution)/shard_map/dot_general | solution.py:114
  37.9 35.0 %all-to-all-done = bf16[256,2,2048]{2,1,0:T(2,128)(2,1)} async-done(((bf16[256,2,2048]{2,1,0:T(2,128)(2,1)}), bf16[256,2,2048]{2,1,0:T(2,128)(2,1)}, u32[]{:S(2)}, u32[]{:S(2)}) %all-to-all-start) | async-done | bytes 2097184 | tf_op jit(solution)/shard_map/all_to_all | solution.py:189
  76.9 17.9 %reshape.677 = bf16[16,32,32,2,32]{4,3,2,0,1:T(2,128)(2,1)} reshape(bf16[16,16,2,2048]{3,0,2,1:T(8,128)(2,1)} %copy.102) | data formatting | bytes 4194304 | tf_op jit(solution)/shard_map/reshape | solution.py:56
  94.8 12.6 %fusion.20 = bf16[16,32,64,2,64]{4,2,1,0,3:T(8,128)(2,1)} fusion(bf16[16,32,32,2,32,1]{4,3,2,0,1,5:T(2,128)(2,1)} %bitcast.203, bf16[1,32,2,64]{3,1,0,2:T(8,128)(2,1)S(1)} %get-tuple-element.59, bf16[1,32,2,64]{3,1,0,2:T(8,128)(2,1)S(1)} %get-tuple-element.58), kind=kOutput, calls=%fused_computation.24 | convolution fusion | flops 811663360 | bytes 10502144 | tf_op jit(solution)/shard_map/blycz,cydm->blmdz/dot_general | solution.py:60
  107.4 28.7 %fusion.1 = (f32[64,64,64]{2,0,1:T(8,128)}, bf16[16,64,64,2,64]{4,1,2,0,3:T(8,128)(2,1)}) fusion(f32[64,64,64]{2,0,1:T(8,128)} %fusion.29, bf16[16,32,64,2,64]{4,2,1,0,3:T(8,128)(2,1)} %fusion.20, bf16[1,32,2,64]{3,1,0,2:T(8,128)(2,1)S(1)} %get-tuple-element.59, bf16[1,32,2,64]{3,1,0,2:T(8,128)(2,1)S(1)} %get-tuple-element.58), kind=kOutput, calls=%fused_computation.3 | convolution fusion | flops 1107066880 | bytes 27279360 | tf_op jit(solution)/shard_map/bxycz,cxdn->bnydz/dot_general | solution.py:70
  136.1 18.9 %fusion.6 = bf16[16,32,64,2,64,1]{4,1,2,0,3,5:T(8,128)(2,1)} fusion(bf16[16,64,64,2,64]{4,1,2,0,3:T(8,128)(2,1)} %get-tuple-element.42, bf16[1,64,2,32]{1,3,0,2:T(8,128)(2,1)S(1)} %get-tuple-element.57, bf16[1,64,2,32]{1,3,0,2:T(8,128)(2,1)S(1)} %get-tuple-element.56), kind=kOutput, calls=%fused_computation.10 | convolution fusion | flops 1077968896 | bytes 25182208 | tf_op jit(solution)/shard_map/bnydz,dncx->bxycz/dot_general | solution.py:76
  155.0 19.3 %convolution_bitcast_fusion = f32[16,32,32,2,32]{4,2,3,1,0:T(8,128)} fusion(bf16[16,32,64,2,64,1]{4,1,2,0,3,5:T(8,128)(2,1)} %fusion.6, bf16[1,64,2,32]{1,3,0,2:T(8,128)(2,1)S(1)} %get-tuple-element.57, bf16[1,64,2,32]{1,3,0,2:T(8,128)(2,1)S(1)} %get-tuple-element.56), kind=kOutput, calls=%fused_computation.25 | convolution fusion | flops 807469056 | bytes 12599296 | tf_op jit(solution)/shard_map/blydn,dnck->blyck/dot_general | solution.py:89
  174.3 28.6 %copy.138 = f32[16,32,32,2,32]{4,3,2,0,1:T(2,128)} copy(f32[16,32,32,2,32]{4,2,3,1,0:T(8,128)} %convolution_bitcast_fusion) | data formatting | bytes 8388608 | tf_op jit(solution)/shard_map/reshape | solution.py:90
  202.9 21.7 %reshape.699 = f32[16,32,2048]{2,0,1:T(8,128)} reshape(f32[16,32,32,2,32]{4,3,2,0,1:T(2,128)} %copy.138) | data formatting | bytes 8388608 | tf_op jit(solution)/shard_map/reshape | solution.py:90
  224.6 10.1 %all-to-all-start.1 = ((f32[16,32,2048]{2,0,1:T(8,128)}), f32[16,32,2048]{2,0,1:T(8,128)}, u32[]{:S(2)}, u32[]{:S(2)}) async-start(f32[16,32,2048]{2,0,1:T(8,128)} %reshape.699), calls=%async_computation.1 | async-start | bytes 8388608 | tf_op jit(solution)/shard_map/all_to_all | solution.py:195
  239.4 5.0 broadcast_multiply_fusion.2
  247.5 5.1 reshape.682
  263.4 12.6 %fusion.14 = f32[64,768]{1,0:T(8,128)S(1)} fusion(f32[64,4096]{1,0:T(8,128)} %div.129, f32[256,4096]{0,1:T(8,128)} %bitcast.212, f32[256,4096]{0,1:T(8,128)} %bitcast.213, f32[256,4096]{0,1:T(8,128)} %bitcast.211), kind=kOutput, calls=%fused_computation.18 | convolution fusion | flops 2422210560 | bytes 13828096 | tf_op jit(solution)/shard_map/dot_general | solution.py:124
  276.2 36.9 %all-to-all-done.1 = f32[16,32,2048]{2,0,1:T(8,128)} async-done(((f32[16,32,2048]{2,0,1:T(8,128)}), f32[16,32,2048]{2,0,1:T(8,128)}, u32[]{:S(2)}, u32[]{:S(2)}) %all-to-all-start.1) | async-done | bytes 4194336 | tf_op jit(solution)/shard_map/all_to_all | solution.py:195
  313.0 5.5 copy.110
  318.5 4.7 copy.109
  323.2 4.0 copy.143
  330.2 15.3 %all-reduce = (f32[256]{0:T(256)S(1)}, f32[256]{0:T(256)S(1)}, f32[3,256]{1,0:T(4,128)S(1)}) all-reduce(f32[256]{0:T(256)S(1)} %get-tuple-element.25, f32[256]{0:T(256)S(1)} %get-tuple-element.24, f32[3,256]{1,0:T(4,128)S(1)} %pad_maximum_fusion.9), channel_id=1, replica_groups=mesh['img'=2,'band'=4,'pw'=4] {'pw'}, use_global_device_ids=true, to_apply=%region_5.6 | all-reduce | flops 1280 | bytes 10240 | tf_op jit(solution)/shard_map/psum | solution.py:203
  345.5 19.3 %all-reduce.1 = (f32[256]{0:T(256)S(1)}, f32[256]{0:T(256)S(1)}, f32[3,256]{1,0:T(4,128)S(1)}) all-reduce(f32[256]{0:T(256)S(1)} %get-tuple-element.29, f32[256]{0:T(256)S(1)} %get-tuple-element.30, f32[3,256]{1,0:T(4,128)S(1)} %get-tuple-element.31), channel_id=1, replica_groups=mesh['img'=2,'band'=4,'pw'=4] {'band'}, use_global_device_ids=true, to_apply=%region_6.7 | all-reduce | flops 1280 | bytes 10240 | tf_op jit(solution)/shard_map/psum | solution.py:202
  366.7 18.0 %all_to_all.36 = f32[256,2,32,2,32]{4,3,2,0,1:T(2,128)} reshape(f32[16,16,2,2048]{3,1,0,2:T(8,128)} %copy.109) | data formatting | bytes 8388608 | tf_op jit(solution)/shard_map/all_to_all | solution.py:195
  384.6 20.8 %copy.114 = f32[256,2,32,2,32]{0,4,3,2,1:T(8,128)} copy(f32[256,2,32,2,32]{4,3,2,0,1:T(2,128)} %all_to_all.36) | data formatting | bytes 8388608 | tf_op jit(solution)/shard_map/all_to_all | solution.py:195
  405.5 4.6 fusion.41
  415.7 8.2 %multiply_bitcast_fusion = f32[1024,512]{0,1:T(8,128)S(1)} fusion(bf16[1024,4096]{1,0:T(8,128)(2,1)} %bitcast.199, bf16[256,4096]{1,0:T(8,128)(2,1)} %copy.115, bf16[256,4096]{1,0:T(8,128)(2,1)} %fusion.41), kind=kOutput, calls=%fused_computation.59 | convolution fusion | flops 4303880192 | bytes 14680064 | tf_op jit(solution)/shard_map/ik,jk->ij/dot_general | solution.py:213
  423.9 97.3 %all-reduce.3 = bf16[1024,512]{0,1:T(8,128)(2,1)} all-reduce(f32[1024,512]{0,1:T(8,128)S(1)} %multiply_bitcast_fusion), channel_id=1, replica_groups=mesh['img'=2,'band'=4,'pw'=4] {'band','pw'}, use_global_device_ids=true, to_apply=%region_7.8 | all-reduce | flops 524288 | bytes 3145728 | tf_op jit(solution)/shard_map/psum | solution.py:216
  521.3 7.2 %fusion.152 = f32[512,4096]{1,0:T(8,128)S(1)} fusion(bf16[1024,512]{0,1:T(8,128)(2,1)} %all-reduce.3, bf16[1024,4096]{1,0:T(8,128)(2,1)} %bitcast.200), kind=kOutput, calls=%fused_computation.217 | convolution fusion | flops 4294967296 | bytes 17825792 | tf_op jit(solution)/shard_map/ij,ik->jk/dot_general | solution.py:217
  532.2 5.6 copy.116
  543.1 5.4 copy.118
  548.5 6.6 %reshape.680 = f32[1,256,2,2048]{3,2,1,0:T(2,128)} reshape(f32[256,4096]{1,0:T(8,128)} %get-tuple-element.43) | data formatting | bytes 8388608 | tf_op jit(solution)/shard_map/reshape | solution.py:218
  555.0 10.7 %fusion.35 = bf16[1,256,2,2048]{3,1,2,0:T(8,128)(2,1)S(1)} fusion(f32[1,256,2,2048]{3,1,2,0:T(8,128)} %copy.118, f32[1,256,2,2048]{3,2,1,0:T(2,128)} %reshape.680, f32[16,16,2,2048]{3,1,0,2:T(8,128)} %copy.109, f32[1,256,2,2048]{3,2,1,0:T(2,128)} %reshape.682, f32[2,2048]{1,0:T(2,128)S(1)} %get-tuple-element.55, f32[256]{0:T(256)S(1)} %add_divide_fusion, ...), kind=kLoop, calls=%fused_computation.43 | loop fusion | flops 10485760 | bytes 18908160 | tf_op jit(solution)/shard_map/convert_element_type | solution.py:221
  (69 shorter events, 46.1 us)
Async XLA Ops:
  0.6 12.1 %copy-start = (bf16[1,1024,256]{2,1,0:T(8,128)(2,1)S(1)}, bf16[1,1024,256]{2,1,0:T(8,128)(2,1)}, u32[]{:S(2)}) copy-start(bf16[1,1024,256]{2,1,0:T(8,128)(2,1)} %param.8) | copy-start | bytes 1572868
  18.5 11.8 %copy-start.9 = (s32[256]{0:T(256)S(1)}, s32[256]{0:T(256)}, u32[]{:S(2)}) copy-start(s32[256]{0:T(256)} %param.12) | copy-start | bytes 3076
  18.5 11.8 %copy-start.10 = (f32[4]{0:T(128)S(1)}, f32[4]{0:T(128)}, u32[]{:S(2)}) copy-start(f32[4]{0:T(128)} %param.13) | copy-start | bytes 52
  18.5 11.9 %copy-start.5 = (s32[1,3,256]{2,0,1:T(1,128)S(1)}, s32[1,3,256]{2,0,1:T(1,128)}, u32[]{:S(2)}) copy-start(s32[1,3,256]{2,0,1:T(1,128)} %param.9) | copy-start | bytes 9220
  21.3 51.6 %all-to-all-start = ((bf16[256,2,2048]{2,1,0:T(2,128)(2,1)}), bf16[256,2,2048]{2,1,0:T(2,128)(2,1)}, u32[]{:S(2)}, u32[]{:S(2)}) async-start(bf16[256,2,2048]{2,1,0:T(2,128)(2,1)} %reshape.676), calls=%async_computation | async-start | bytes 4194304 | tf_op jit(solution)/shard_map/all_to_all | solution.py:189
  224.6 88.5 %all-to-all-start.1 = ((f32[16,32,2048]{2,0,1:T(8,128)}), f32[16,32,2048]{2,0,1:T(8,128)}, u32[]{:S(2)}, u32[]{:S(2)}) async-start(f32[16,32,2048]{2,0,1:T(8,128)} %reshape.699), calls=%async_computation.1 | async-start | bytes 8388608 | tf_op jit(solution)/shard_map/all_to_all | solution.py:195
  234.7 18.0 %collective-permute-start = (s32[3,256]{1,0:T(4,128)S(1)}, s32[3,256]{1,0:T(4,128)S(1)}, u32[]{:S(2)}, u32[]{:S(2)}) collective-permute-start(s32[3,256]{1,0:T(4,128)S(1)} %bitcast.224), channel_id=1, source_target_pairs={{16,0},{17,1},{18,2},{19,3},{20,4},{21,5},{22,6},{23,7},{24,8},{25... | collective-permute-start | bytes 9224 | tf_op jit(solution)/shard_map/ppermute | solution.py:22
  236.0 16.7 %collective-permute-start.1 = (s32[3,256]{1,0:T(4,128)S(1)}, s32[3,256]{1,0:T(4,128)S(1)}, u32[]{:S(2)}, u32[]{:S(2)}) collective-permute-start(s32[3,256]{1,0:T(4,128)S(1)} %bitcast.225), channel_id=1, source_target_pairs={{0,16},{1,17},{2,18},{3,19},{4,20},{5,21},{6,22},{7,23},{8,24},{9,... | collective-permute-start | bytes 9224 | tf_op jit(solution)/shard_map/ppermute | solution.py:22
  247.5 5.2 copy-start.7
  247.5 5.2 copy-start.8
  327.2 1.9 copy-start.2
  405.5 149.6 %copy-start.6 = (f32[256]{0:T(256)}, f32[256]{0:T(256)S(1)}, u32[]{:S(2)}) copy-start(f32[256]{0:T(256)S(1)} %add_divide_fusion) | copy-start | bytes 3076
  405.5 4.7 copy-start.3
  405.5 5.5 copy-start.4
  555.0 14.2 %copy-start.1 = (bf16[1,1024,256]{2,1,0:T(8,128)(2,1)S(1)}, bf16[1,1024,256]{2,1,0:T(8,128)(2,1)}, u32[]{:S(2)}) copy-start(bf16[1,1024,256]{2,1,0:T(8,128)(2,1)} %param.8) | copy-start | bytes 1572868
